TPU v7x, 128 devices: a whole 4x4x4 slice. The times are simulated.
128 devices in a mesh: ctx: 128 (over x, y, z, core).
Axes of the slice: x: 4, y: 4, z: 4, core: 2. Of those that a mesh axis runs over, the one named last changes fastest.
Arguments:
- queries: bfloat16 [32768, 2048], P('ctx')
- keys: bfloat16 [32768, 512], P('ctx')
- values: bfloat16 [32768, 512], P('ctx'), may hold values from -6 to 6
- cotangent: bfloat16 [32768, 2048], P('ctx'), may hold values from -180 to 180
- summary_positions: int32 [256], replicated, may hold values from 0 to 32767, as said below
Outputs:
- query_grad: bfloat16 [32768, 2048], P('ctx')
- key_grad: bfloat16 [32768, 512], P('ctx')
- value_gradient: bfloat16 [32768, 512], P('ctx')
Inputs may be any that keep to these rules, and one draw needn't show every extreme that they name: `summary_positions`: entry m lies in [m * 128, (m + 1) * 128); the first entry is 0 and the last is 32767.
All inputs are finite; a program needn't handle non-finite values.
Results may differ from a plain program's by a relative error of at most 0.012.
The roundings to bfloat16 on the way count: a program that leaves them out, or rounds other values in their place, can miss the bound.
Values may be sent and summed in bfloat16 or wider, within the bound.
No kernel may reach another device: no remote copies, remote signals or barrier semaphores. Data moves between devices by JAX's collectives and lax.ppermute only.
A program may use at most 128 MiB of HBM per device.

v0:
```python
import jax
import jax.numpy as jnp
from jax import lax
from jax.sharding import PartitionSpec as P

HEAD = 128
BAND_LENGTH = 1024
NEGATIVE = -1e30


def passed_along(block, axis, distance):
    devices = range(lax.axis_size(axis))
    route = [(i - distance, i) for i in devices if i - distance in devices]
    return lax.ppermute(block, axis, route)


def group_pass(
    group_query, group_cot, band_keys, band_vals, summ_keys, summ_vals, band_mask, summ_mask, scale
):
    band_score = (
        jnp.einsum("tgd,kd->gtk", group_query, band_keys, preferred_element_type=jnp.float32)
        * scale
    )
    band_score = jnp.where(band_mask[None], band_score, NEGATIVE)
    summ_score = (
        jnp.einsum("tgd,kd->gtk", group_query, summ_keys, preferred_element_type=jnp.float32)
        * scale
    )
    summ_score = jnp.where(summ_mask[None], summ_score, NEGATIVE)
    highest = jnp.maximum(jnp.max(band_score, -1), jnp.max(summ_score, -1))
    total = jnp.sum(jnp.exp(band_score - highest[..., None]), -1) + jnp.sum(
        jnp.exp(summ_score - highest[..., None]), -1
    )
    log_total = highest + jnp.log(total)
    band_prob = jnp.exp(band_score - log_total[..., None])
    summ_prob = jnp.exp(summ_score - log_total[..., None])
    band_half = band_prob.astype(jnp.bfloat16)
    summ_half = summ_prob.astype(jnp.bfloat16)
    attended = jnp.einsum("gtk,kd->tgd", band_half, band_vals, preferred_element_type=jnp.float32)
    attended = attended + jnp.einsum(
        "gtk,kd->tgd", summ_half, summ_vals, preferred_element_type=jnp.float32
    )
    attended = lax.optimization_barrier(attended.astype(jnp.bfloat16)).astype(jnp.float32)
    delta = jnp.sum(group_cot.astype(jnp.float32) * attended, -1).T
    band_dprob = jnp.einsum("tgd,kd->gtk", group_cot, band_vals, preferred_element_type=jnp.float32)
    summ_dprob = jnp.einsum("tgd,kd->gtk", group_cot, summ_vals, preferred_element_type=jnp.float32)
    band_dscore = (band_prob * (band_dprob - delta[..., None])).astype(jnp.bfloat16)
    summ_dscore = (summ_prob * (summ_dprob - delta[..., None])).astype(jnp.bfloat16)
    query_part = jnp.einsum(
        "gtk,kd->tgd", band_dscore, band_keys, preferred_element_type=jnp.float32
    )
    query_part = (
        query_part
        + jnp.einsum("gtk,kd->tgd", summ_dscore, summ_keys, preferred_element_type=jnp.float32)
    ) * scale
    key_part = (
        jnp.einsum("gtk,tgd->kd", band_dscore, group_query, preferred_element_type=jnp.float32)
        * scale
    )
    value_part = jnp.einsum("gtk,tgd->kd", band_half, group_cot, preferred_element_type=jnp.float32)
    summ_key_part = (
        jnp.einsum("gtk,tgd->kd", summ_dscore, group_query, preferred_element_type=jnp.float32)
        * scale
    )
    summ_value_part = jnp.einsum(
        "gtk,tgd->kd", summ_half, group_cot, preferred_element_type=jnp.float32
    )
    return (query_part, key_part, value_part, summ_key_part, summ_value_part, log_total, delta)


def body(queries, keys, values, cotangent, summary_positions):
    row_count = queries.shape[0]
    key_cols = keys.shape[1]
    kv_heads = key_cols // HEAD
    group = queries.shape[1] // key_cols
    scale = HEAD ** (-0.5)
    reach = BAND_LENGTH // row_count
    device_count = lax.axis_size("ctx")
    shard_index = lax.axis_index("ctx")
    first_row = shard_index * row_count
    per_device = summary_positions.shape[0] // device_count
    earlier_keys, earlier_vals = ([], [])
    for turn in range(reach):
        prev_keys, prev_vals = passed_along((keys, values), "ctx", reach - turn)
        earlier_keys.append(prev_keys)
        earlier_vals.append(prev_vals)
    band_keys = jnp.concatenate(earlier_keys + [keys], 0)
    band_vals = jnp.concatenate(earlier_vals + [values], 0)
    local_rows = (
        lax.dynamic_slice_in_dim(summary_positions, shard_index * per_device, per_device, 0)
        - first_row
    )
    local_keys = jnp.take(keys, local_rows, axis=0)
    local_vals = jnp.take(values, local_rows, axis=0)
    summ_keys, summ_vals = (
        lax.all_gather(local_keys, "ctx", axis=0, tiled=True),
        lax.all_gather(local_vals, "ctx", axis=0, tiled=True),
    )
    query_pos = first_row + jnp.arange(row_count, dtype=jnp.int32)
    band_pos = first_row - BAND_LENGTH + jnp.arange(BAND_LENGTH + row_count, dtype=jnp.int32)
    distance = query_pos[:, None] - band_pos[None, :]
    band_mask = (distance >= 0) & (distance < BAND_LENGTH) & (band_pos[None, :] >= 0)
    summ_mask = summary_positions[None, :] <= query_pos[:, None]
    query_parts, key_parts, value_parts, summ_kparts, summ_vparts, lse_parts, delta_parts = (
        [],
        [],
        [],
        [],
        [],
        [],
        [],
    )
    for head_group in range(kv_heads):
        query_cols = slice(head_group * group * HEAD, (head_group + 1) * group * HEAD)
        head_cols = slice(head_group * HEAD, (head_group + 1) * HEAD)
        group_query = queries[:, query_cols].reshape(row_count, group, HEAD)
        group_cot = cotangent[:, query_cols].reshape(row_count, group, HEAD)
        outcome = group_pass(
            group_query,
            group_cot,
            band_keys[:, head_cols],
            band_vals[:, head_cols],
            summ_keys[:, head_cols],
            summ_vals[:, head_cols],
            band_mask,
            summ_mask,
            scale,
        )
        query_parts.append(outcome[0].reshape(row_count, group * HEAD))
        key_parts.append(outcome[1])
        value_parts.append(outcome[2])
        summ_kparts.append(outcome[3])
        summ_vparts.append(outcome[4])
        lse_parts.append(outcome[5])
        delta_parts.append(outcome[6])
    query_grad = jnp.concatenate(query_parts, 1).astype(jnp.bfloat16)
    band_kgrad = jnp.concatenate(key_parts, 1)
    band_vgrad = jnp.concatenate(value_parts, 1)
    key_grad = band_kgrad[BAND_LENGTH:]
    value_gradient = band_vgrad[BAND_LENGTH:]
    for turn in range(reach):
        lower = turn * row_count
        back_keys, back_vals = (
            passed_along(
                band_kgrad[lower : lower + row_count].astype(jnp.bfloat16), "ctx", turn - reach
            ).astype(jnp.float32),
            passed_along(
                band_vgrad[lower : lower + row_count].astype(jnp.bfloat16), "ctx", turn - reach
            ).astype(jnp.float32),
        )
        key_grad = key_grad + back_keys
        value_gradient = value_gradient + back_vals
    summ_kterm = jnp.concatenate(summ_kparts, 1)
    summ_vterm = jnp.concatenate(summ_vparts, 1)
    share_keys, share_vals = (
        lax.psum_scatter(summ_kterm, "ctx", scatter_dimension=0, tiled=True),
        lax.psum_scatter(summ_vterm, "ctx", scatter_dimension=0, tiled=True),
    )
    key_grad = key_grad.at[local_rows].add(share_keys)
    value_gradient = value_gradient.at[local_rows].add(share_vals)
    return (query_grad, key_grad.astype(jnp.bfloat16), value_gradient.astype(jnp.bfloat16))


def solution(mesh):
    return jax.shard_map(
        body,
        mesh=mesh,
        in_specs=(P("ctx", None), P("ctx", None), P("ctx", None), P("ctx", None), P()),
        out_specs=(P("ctx", None), P("ctx", None), P("ctx", None)),
        check_vma=False,
    )
```

profile of v0, /device:TPU:1, one launch (start us, length us, event | category | flops | bytes accessed | tf_op | source)
XLA Modules:
  0.0 388.8 jit_solution(9783124111173024778)
XLA Ops:
  7.2 4.9 %collective-permute-start.3 = (bf16[256,512]{1,0:T(8,128)(2,1)}, bf16[256,512]{1,0:T(8,128)(2,1)}, u32[]{:S(2)}, u32[]{:S(2)}) collective-permute-start(bf16[256,512]{1,0:T(8,128)(2,1)} %param.8), channel_id=1, source_target_pairs={{0,1},{1,2},{2,3},{3,4},{4,5},{5,6},{6,7},{7,8},{8,9},{9,10},{10,1... | collective-permute-start | bytes 786440 | tf_op jit(solution)/shard_map/ppermute | solution.py:14
  12.2 4.2 %collective-permute-start.2 = (bf16[256,512]{1,0:T(8,128)(2,1)}, bf16[256,512]{1,0:T(8,128)(2,1)}, u32[]{:S(2)}, u32[]{:S(2)}) collective-permute-start(bf16[256,512]{1,0:T(8,128)(2,1)} %param.8), channel_id=1, source_target_pairs={{0,2},{1,3},{2,4},{3,5},{4,6},{5,7},{6,8},{7,9},{8,10},{9,11},{10,... | collective-permute-start | bytes 786440 | tf_op jit(solution)/shard_map/ppermute | solution.py:14
  16.4 3.3 collective-permute-start.6
  19.7 2.7 collective-permute-start.5
  22.4 4.3 %collective-permute-start.4 = (bf16[256,512]{1,0:T(8,128)(2,1)}, bf16[256,512]{1,0:T(8,128)(2,1)}, u32[]{:S(2)}, u32[]{:S(2)}) collective-permute-start(bf16[256,512]{1,0:T(8,128)(2,1)} %param.9), channel_id=1, source_target_pairs={{0,4},{1,5},{2,6},{3,7},{4,8},{5,9},{6,10},{7,11},{8,12},{9,13},{1... | collective-permute-start | bytes 786440 | tf_op jit(solution)/shard_map/ppermute | solution.py:14
  27.5 1.5 gather_fusion.1
  29.0 1.5 gather_fusion
  31.5 41.0 %all-gather = bf16[128,2,512]{2,1,0:T(2,128)(2,1)S(1)} all-gather(bf16[1,2,512]{2,1,0:T(2,128)(2,1)S(1)} %get-tuple-element.28), channel_id=1, replica_groups=mesh['ctx'=128] {'ctx'}, dimensions={0}, use_global_device_ids=true | all-gather | bytes 264192 | tf_op jit(solution)/shard_map/all_gather | solution.py:96
  72.6 1.4 fusion.98
  75.6 1.3 fusion.103
  76.9 1.4 fusion.107
  78.3 1.6 fusion.33
  80.7 33.2 %all-gather.1 = bf16[128,2,512]{2,1,0:T(2,128)(2,1)S(1)} all-gather(bf16[1,2,512]{2,1,0:T(2,128)(2,1)S(1)} %get-tuple-element.27), channel_id=1, replica_groups=mesh['ctx'=128] {'ctx'}, dimensions={0}, use_global_device_ids=true | all-gather | bytes 264192 | tf_op jit(solution)/shard_map/all_gather | solution.py:97
  114.3 1.1 copy.343
  115.4 1.1 copy.349
  116.6 3.0 collective-permute-start.7
  120.6 2.6 collective-permute-start.1
  124.1 4.5 %collective-permute-start = (bf16[256,512]{1,0:T(8,128)(2,1)}, bf16[256,512]{1,0:T(8,128)(2,1)S(1)}, u32[]{:S(2)}, u32[]{:S(2)}) collective-permute-start(bf16[256,512]{1,0:T(8,128)(2,1)} %param.8), channel_id=1, source_target_pairs={{0,4},{1,5},{2,6},{3,7},{4,8},{5,9},{6,10},{7,11},{8,12},{9,13},{1... | collective-permute-start | bytes 786440 | tf_op jit(solution)/shard_map/ppermute | solution.py:14
  130.6 3.3 collective-permute-done
  139.2 1.0 fusion.50
  141.4 1.0 convolution_bitcast_fusion
  142.4 1.1 fusion.1
  146.7 1.0 fusion.52
  149.1 1.1 fusion.89
  150.2 1.0 convolution_bitcast_fusion.2
  151.2 1.1 fusion.5
  152.3 1.2 fusion.102
  155.9 1.0 fusion.51
  158.4 1.0 fusion.90
  159.4 1.0 convolution_bitcast_fusion.1
  160.4 1.1 fusion.3
  162.5 1.0 copy-done.3
  164.8 1.0 convolution_bitcast_fusion.15
  165.8 1.0 fusion.53
  168.1 1.1 fusion.88
  169.2 1.0 convolution_bitcast_fusion.3
  170.2 1.1 fusion.7
  173.3 1.2 fusion.13
  175.5 1.2 fusion.95
  176.7 1.7 pad_maximum_fusion
  178.3 1.2 fusion.94
  179.6 1.7 pad_maximum_fusion.1
  182.7 1.5 fusion.43
  185.1 2.6 fusion.44
  188.6 1.5 fusion.42
  190.3 2.3 fusion.97
  192.6 1.3 collective-permute-start.8
  193.9 3.5 collective-permute-start.11
  197.4 1.3 collective-permute-start.10
  198.7 1.4 collective-permute-start.9
  200.2 1.0 fusion.96
  201.2 1.4 collective-permute-start.12
  202.7 2.0 pad_maximum_fusion.3
  204.7 1.1 pad_maximum_fusion.2
  206.2 2.7 collective-permute-start.15
  208.9 5.6 %collective-permute-done.11 = bf16[256,512]{0,1:T(8,128)(2,1)} collective-permute-done((bf16[256,512]{0,1:T(8,128)(2,1)}, bf16[256,512]{0,1:T(8,128)(2,1)}, u32[]{:S(2)}, u32[]{:S(2)}) %collective-permute-start.11) | collective-permute-done | bytes 262176 | tf_op jit(solution)/shard_map/ppermute | solution.py:14
  214.5 1.3 collective-permute-start.14
  215.8 1.3 collective-permute-start.13
  217.1 1.5 fusion.75
  218.8 15.7 %collective-permute-done.15 = bf16[256,512]{0,1:T(8,128)(2,1)S(1)} collective-permute-done((bf16[256,512]{0,1:T(8,128)(2,1)}, bf16[256,512]{0,1:T(8,128)(2,1)S(1)}, u32[]{:S(2)}, u32[]{:S(2)}) %collective-permute-start.15) | collective-permute-done | bytes 262176 | tf_op jit(solution)/shard_map/ppermute | solution.py:14
  235.0 1.2 fusion.72
  236.4 140.0 %all-reduce.5.cloned.1.call-done = (f32[256,512]{0,1:T(8,128)}, f32[256,512]{0,1:T(8,128)}) async-done(((f32[256,512]{0,1:T(8,128)}, f32[256,512]{0,1:T(8,128)}), (f32[256,512]{0,1:T(8,128)}, f32[256,512]{0,1:T(8,128)})) %all-reduce.5.cloned.1.call-update) | async-done | bytes 1048592
  376.4 1.1 constant_dynamic-slice_fusion.1
  377.5 1.1 constant_dynamic-slice_fusion
  (165 shorter events, 37.4 us)
Async XLA Ops:
  7.2 369.2 %all-reduce.5.cloned.1.call-start = ((), (), s32[]{:S(2)}) async-start(), calls=%async_computation | async-start | bytes 2097152
  7.2 127.8 %collective-permute-start.3 = (bf16[256,512]{1,0:T(8,128)(2,1)}, bf16[256,512]{1,0:T(8,128)(2,1)}, u32[]{:S(2)}, u32[]{:S(2)}) collective-permute-start(bf16[256,512]{1,0:T(8,128)(2,1)} %param.8), channel_id=1, source_target_pairs={{0,1},{1,2},{2,3},{3,4},{4,5},{5,6},{6,7},{7,8},{8,9},{9,10},{10,1... | collective-permute-start | bytes 786440 | tf_op jit(solution)/shard_map/ppermute | solution.py:14
  12.2 121.8 %collective-permute-start.2 = (bf16[256,512]{1,0:T(8,128)(2,1)}, bf16[256,512]{1,0:T(8,128)(2,1)}, u32[]{:S(2)}, u32[]{:S(2)}) collective-permute-start(bf16[256,512]{1,0:T(8,128)(2,1)} %param.8), channel_id=1, source_target_pairs={{0,2},{1,3},{2,4},{3,5},{4,6},{5,7},{6,8},{7,9},{8,10},{9,11},{10,... | collective-permute-start | bytes 786440 | tf_op jit(solution)/shard_map/ppermute | solution.py:14
  16.4 107.7 %collective-permute-start.6 = (bf16[256,512]{1,0:T(8,128)(2,1)}, bf16[256,512]{1,0:T(8,128)(2,1)}, u32[]{:S(2)}, u32[]{:S(2)}) collective-permute-start(bf16[256,512]{1,0:T(8,128)(2,1)} %param.9), channel_id=1, source_target_pairs={{0,2},{1,3},{2,4},{3,5},{4,6},{5,7},{6,8},{7,9},{8,10},{9,11},{10,... | collective-permute-start | bytes 786440 | tf_op jit(solution)/shard_map/ppermute | solution.py:14
  19.7 100.9 %collective-permute-start.5 = (bf16[256,512]{1,0:T(8,128)(2,1)}, bf16[256,512]{1,0:T(8,128)(2,1)}, u32[]{:S(2)}, u32[]{:S(2)}) collective-permute-start(bf16[256,512]{1,0:T(8,128)(2,1)} %param.9), channel_id=1, source_target_pairs={{0,3},{1,4},{2,5},{3,6},{4,7},{5,8},{6,9},{7,10},{8,11},{9,12},{10... | collective-permute-start | bytes 786440 | tf_op jit(solution)/shard_map/ppermute | solution.py:14
  22.4 94.2 %collective-permute-start.4 = (bf16[256,512]{1,0:T(8,128)(2,1)}, bf16[256,512]{1,0:T(8,128)(2,1)}, u32[]{:S(2)}, u32[]{:S(2)}) collective-permute-start(bf16[256,512]{1,0:T(8,128)(2,1)} %param.9), channel_id=1, source_target_pairs={{0,4},{1,5},{2,6},{3,7},{4,8},{5,9},{6,10},{7,11},{8,12},{9,13},{1... | collective-permute-start | bytes 786440 | tf_op jit(solution)/shard_map/ppermute | solution.py:14
  72.6 4.3 %copy-start.16 = (bf16[256,512]{1,0:T(8,128)(2,1)}, bf16[256,512]{1,0:T(8,128)(2,1)S(1)}, u32[]{:S(2)}) copy-start(bf16[256,512]{1,0:T(8,128)(2,1)S(1)} %reshape.253) | copy-start | bytes 786436
  74.1 2.7 copy-start.6
  74.3 2.6 copy-start.8
  74.4 3.8 copy-start.10
  74.6 0.7 copy-start.12
  75.3 4.6 %copy-start.22 = (bf16[256,2048]{1,0:T(8,128)(2,1)S(1)}, bf16[256,2048]{1,0:T(8,128)(2,1)}, u32[]{:S(2)}) copy-start(bf16[256,2048]{1,0:T(8,128)(2,1)} %param.10) | copy-start | bytes 3145732
  114.1 33.8 %copy-start.18 = (bf16[256,512]{1,0:T(8,128)(2,1)}, bf16[256,512]{1,0:T(8,128)(2,1)S(1)}, u32[]{:S(2)}) copy-start(bf16[256,512]{1,0:T(8,128)(2,1)S(1)} %reshape.255) | copy-start | bytes 786436
  116.5 19.4 %copy-start.32 = (bf16[256,512]{1,0:T(8,128)(2,1)S(1)}, bf16[256,512]{1,0:T(8,128)(2,1)}, u32[]{:S(2)}) copy-start(bf16[256,512]{1,0:T(8,128)(2,1)} %param.8) | copy-start | bytes 786436
  116.5 19.4 %copy-start.5 = (pred[256,1280]{0,1:T(8,128)(4,1)S(1)}, pred[256,1280]{0,1:T(8,128)(4,1)}, u32[]{:S(2)}) copy-start(pred[256,1280]{0,1:T(8,128)(4,1)} %fusion.33) | copy-start | bytes 983044
  116.6 19.4 %copy-start.13 = (bf16[256,512]{0,1:T(8,128)(2,1)S(1)}, bf16[256,512]{0,1:T(8,128)(2,1)}, u32[]{:S(2)}) copy-start(bf16[256,512]{0,1:T(8,128)(2,1)} %copy-done.12) | copy-start | bytes 786436
  116.6 13.0 %collective-permute-start.7 = (bf16[256,512]{1,0:T(8,128)(2,1)}, bf16[256,512]{1,0:T(8,128)(2,1)S(1)}, u32[]{:S(2)}, u32[]{:S(2)}) collective-permute-start(bf16[256,512]{1,0:T(8,128)(2,1)} %param.9), channel_id=1, source_target_pairs={{0,1},{1,2},{2,3},{3,4},{4,5},{5,6},{6,7},{7,8},{8,9},{9,10},{10,1... | collective-permute-start | bytes 786440 | tf_op jit(solution)/shard_map/ppermute | solution.py:14
  120.6 13.4 %collective-permute-start.1 = (bf16[256,512]{1,0:T(8,128)(2,1)}, bf16[256,512]{1,0:T(8,128)(2,1)S(1)}, u32[]{:S(2)}, u32[]{:S(2)}) collective-permute-start(bf16[256,512]{1,0:T(8,128)(2,1)} %param.8), channel_id=1, source_target_pairs={{0,3},{1,4},{2,5},{3,6},{4,7},{5,8},{6,9},{7,10},{8,11},{9,12},{10... | collective-permute-start | bytes 786440 | tf_op jit(solution)/shard_map/ppermute | solution.py:14
  124.1 9.8 %collective-permute-start = (bf16[256,512]{1,0:T(8,128)(2,1)}, bf16[256,512]{1,0:T(8,128)(2,1)S(1)}, u32[]{:S(2)}, u32[]{:S(2)}) collective-permute-start(bf16[256,512]{1,0:T(8,128)(2,1)} %param.8), channel_id=1, source_target_pairs={{0,4},{1,5},{2,6},{3,7},{4,8},{5,9},{6,10},{7,11},{8,12},{9,13},{1... | collective-permute-start | bytes 786440 | tf_op jit(solution)/shard_map/ppermute | solution.py:14
  136.0 45.3 %copy-start.14 = (bf16[1280,512]{1,0:T(8,128)(2,1)}, bf16[1280,512]{1,0:T(8,128)(2,1)S(1)}, u32[]{:S(2)}) copy-start(bf16[1280,512]{1,0:T(8,128)(2,1)S(1)} %constant_dynamic-update-slice_fusion) | copy-start | bytes 3932164
  140.2 1.0 copy-start.17
  142.4 1.1 copy-start.11
  151.2 1.1 copy-start.9
  152.3 1.2 copy-start.4
  153.7 1.0 copy-start.19
  160.4 1.1 copy-start.7
  161.5 11.7 %copy-start = (bf16[4,256,1280]{1,2,0:T(8,128)(2,1)}, bf16[4,256,1280]{1,2,0:T(8,128)(2,1)S(1)}, u32[]{:S(2)}) copy-start(bf16[4,256,1280]{1,2,0:T(8,128)(2,1)S(1)} %fusion.3) | copy-start | bytes 7864324
  161.5 2.0 copy-start.3
  171.3 3.2 copy-start.1
  181.3 1.4 copy-start.20
  184.2 4.4 %copy-start.2 = (bf16[4,256,1280]{1,2,0:T(8,128)(2,1)S(1)}, bf16[4,256,1280]{1,2,0:T(8,128)(2,1)}, u32[]{:S(2)}) copy-start(bf16[4,256,1280]{1,2,0:T(8,128)(2,1)} %copy-done.1) | copy-start | bytes 7864324
  184.2 4.4 %copy-start.21 = (f32[128,4,256]{2,0,1:T(8,128)S(1)}, f32[128,4,256]{2,0,1:T(8,128)}, u32[]{:S(2)}) copy-start(f32[128,4,256]{2,0,1:T(8,128)} %fusion.88) | copy-start | bytes 1572868
  190.1 10.1 %copy-start.15 = (bf16[1280,512]{0,1:T(8,128)(2,1)S(1)}, bf16[1280,512]{0,1:T(8,128)(2,1)}, u32[]{:S(2)}) copy-start(bf16[1280,512]{0,1:T(8,128)(2,1)} %fusion.94) | copy-start | bytes 3932164
  190.1 12.5 %copy-start.26 = (f32[256,128]{0,1:T(8,128)S(1)}, f32[256,128]{0,1:T(8,128)}, u32[]{:S(2)}) copy-start(f32[256,128]{0,1:T(8,128)} %fusion.55) | copy-start | bytes 393220
  190.1 12.5 %copy-start.27 = (f32[256,128]{0,1:T(8,128)S(1)}, f32[256,128]{0,1:T(8,128)}, u32[]{:S(2)}) copy-start(f32[256,128]{0,1:T(8,128)} %fusion.56) | copy-start | bytes 393220
  190.1 12.5 %copy-start.28 = (f32[256,128]{0,1:T(8,128)S(1)}, f32[256,128]{0,1:T(8,128)}, u32[]{:S(2)}) copy-start(f32[256,128]{0,1:T(8,128)} %fusion.54) | copy-start | bytes 393220
  190.1 12.5 %copy-start.29 = (f32[256,128]{0,1:T(8,128)S(1)}, f32[256,128]{0,1:T(8,128)}, u32[]{:S(2)}) copy-start(f32[256,128]{0,1:T(8,128)} %convolution_bitcast_fusion.12) | copy-start | bytes 393220
  190.1 12.5 %copy-start.30 = (f32[256,128]{0,1:T(8,128)S(1)}, f32[256,128]{0,1:T(8,128)}, u32[]{:S(2)}) copy-start(f32[256,128]{0,1:T(8,128)} %convolution_bitcast_fusion.14) | copy-start | bytes 393220
  190.2 12.5 %copy-start.31 = (f32[256,128]{0,1:T(8,128)S(1)}, f32[256,128]{0,1:T(8,128)}, u32[]{:S(2)}) copy-start(f32[256,128]{0,1:T(8,128)} %convolution_bitcast_fusion.13) | copy-start | bytes 393220
  192.6 13.6 %collective-permute-start.8 = (bf16[256,512]{0,1:T(8,128)(2,1)}, bf16[256,512]{0,1:T(8,128)(2,1)}, u32[]{:S(2)}, u32[]{:S(2)}) collective-permute-start(bf16[256,512]{0,1:T(8,128)(2,1)} %get-tuple-element.15), channel_id=1, source_target_pairs={{4,0},{5,1},{6,2},{7,3},{8,4},{9,5},{10,6},{11,7},{12,8},{13,9},{1... | collective-permute-start | bytes 786440 | tf_op jit(solution)/shard_map/ppermute | solution.py:14
  193.9 20.6 %collective-permute-start.11 = (bf16[256,512]{0,1:T(8,128)(2,1)}, bf16[256,512]{0,1:T(8,128)(2,1)}, u32[]{:S(2)}, u32[]{:S(2)}) collective-permute-start(bf16[256,512]{0,1:T(8,128)(2,1)} %get-tuple-element.16), channel_id=1, source_target_pairs={{1,0},{2,1},{3,2},{4,3},{5,4},{6,5},{7,6},{8,7},{9,8},{10,9},{11,1... | collective-permute-start | bytes 786440 | tf_op jit(solution)/shard_map/ppermute | solution.py:14
  197.4 18.4 %collective-permute-start.10 = (bf16[256,512]{0,1:T(8,128)(2,1)}, bf16[256,512]{0,1:T(8,128)(2,1)}, u32[]{:S(2)}, u32[]{:S(2)}) collective-permute-start(bf16[256,512]{0,1:T(8,128)(2,1)} %get-tuple-element.17), channel_id=1, source_target_pairs={{2,0},{3,1},{4,2},{5,3},{6,4},{7,5},{8,6},{9,7},{10,8},{11,9},{12,... | collective-permute-start | bytes 786440 | tf_op jit(solution)/shard_map/ppermute | solution.py:14
  198.7 6.0 %copy-start.23 = (bf16[256,512]{1,0:T(8,128)(2,1)S(1)}, bf16[256,512]{1,0:T(8,128)(2,1)}, u32[]{:S(2)}) copy-start(bf16[256,512]{1,0:T(8,128)(2,1)} %copy.234) | copy-start | bytes 786436
  198.7 6.0 %copy-start.24 = (bf16[256,512]{1,0:T(8,128)(2,1)S(1)}, bf16[256,512]{1,0:T(8,128)(2,1)}, u32[]{:S(2)}) copy-start(bf16[256,512]{1,0:T(8,128)(2,1)} %copy.232) | copy-start | bytes 786436
  198.7 6.0 %copy-start.25 = (bf16[256,512]{1,0:T(8,128)(2,1)S(1)}, bf16[256,512]{1,0:T(8,128)(2,1)}, u32[]{:S(2)}) copy-start(bf16[256,512]{1,0:T(8,128)(2,1)} %copy.233) | copy-start | bytes 786436
  198.7 18.4 %collective-permute-start.9 = (bf16[256,512]{0,1:T(8,128)(2,1)}, bf16[256,512]{0,1:T(8,128)(2,1)}, u32[]{:S(2)}, u32[]{:S(2)}) collective-permute-start(bf16[256,512]{0,1:T(8,128)(2,1)} %get-tuple-element.18), channel_id=1, source_target_pairs={{3,0},{4,1},{5,2},{6,3},{7,4},{8,5},{9,6},{10,7},{11,8},{12,9},{13... | collective-permute-start | bytes 786440 | tf_op jit(solution)/shard_map/ppermute | solution.py:14
  201.2 14.6 %copy-start.33 = (bf16[256,512]{0,1:T(8,128)(2,1)S(1)}, bf16[256,512]{0,1:T(8,128)(2,1)}, u32[]{:S(2)}) copy-start(bf16[256,512]{0,1:T(8,128)(2,1)} %get-tuple-element.14) | copy-start | bytes 786436
  201.2 17.6 %collective-permute-start.12 = (bf16[256,512]{0,1:T(8,128)(2,1)}, bf16[256,512]{0,1:T(8,128)(2,1)S(1)}, u32[]{:S(2)}, u32[]{:S(2)}) collective-permute-start(bf16[256,512]{0,1:T(8,128)(2,1)} %get-tuple-element.11), channel_id=1, source_target_pairs={{4,0},{5,1},{6,2},{7,3},{8,4},{9,5},{10,6},{11,7},{12,8},{13,9},{1... | collective-permute-start | bytes 786440 | tf_op jit(solution)/shard_map/ppermute | solution.py:14
  206.2 28.4 %collective-permute-start.15 = (bf16[256,512]{0,1:T(8,128)(2,1)}, bf16[256,512]{0,1:T(8,128)(2,1)S(1)}, u32[]{:S(2)}, u32[]{:S(2)}) collective-permute-start(bf16[256,512]{0,1:T(8,128)(2,1)} %get-tuple-element.12), channel_id=1, source_target_pairs={{1,0},{2,1},{3,2},{4,3},{5,4},{6,5},{7,6},{8,7},{9,8},{10,9},{11,1... | collective-permute-start | bytes 786440 | tf_op jit(solution)/shard_map/ppermute | solution.py:14
  214.5 20.5 %collective-permute-start.14 = (bf16[256,512]{0,1:T(8,128)(2,1)}, bf16[256,512]{0,1:T(8,128)(2,1)S(1)}, u32[]{:S(2)}, u32[]{:S(2)}) collective-permute-start(bf16[256,512]{0,1:T(8,128)(2,1)} %get-tuple-element.13), channel_id=1, source_target_pairs={{2,0},{3,1},{4,2},{5,3},{6,4},{7,5},{8,6},{9,7},{10,8},{11,9},{12,... | collective-permute-start | bytes 786440 | tf_op jit(solution)/shard_map/ppermute | solution.py:14
  215.8 19.2 %collective-permute-start.13 = (bf16[256,512]{0,1:T(8,128)(2,1)S(1)}, bf16[256,512]{0,1:T(8,128)(2,1)S(1)}, u32[]{:S(2)}, u32[]{:S(2)}) collective-permute-start(bf16[256,512]{0,1:T(8,128)(2,1)S(1)} %copy-done.33), channel_id=1, source_target_pairs={{3,0},{4,1},{5,2},{6,3},{7,4},{8,5},{9,6},{10,7},{11,8},{12,9},{13... | collective-permute-start | bytes 786440 | tf_op jit(solution)/shard_map/ppermute | solution.py:14
Sparse Core Ops, SparseCore 0:
  204.8 171.5 all-reduce.4
where the time goes:
time: 390 us; the launch traced here: 389 us
  waiting for transfers between devices  165 us (42%)
  blocking collectives  74.2 us (19%)
  starting transfers between devices  43.8 us (11%)
  matrix products  43.2 us (11%)
  local copies, waits for them, and re-layouts  25.2 us (6%)
  other arithmetic  21.8 us (6%)
  between operations  15.2 us (4%)
    unnamed x2, waiting for transfers between devices  140 us
    ppermute x16, starting transfers between devices, passed_along(): return lax.ppermute(block, axis, route)  43.7 us
    all_gather x1, blocking collectives, body(): lax.all_gather(local_keys, 'ctx', axis=0, tiled=True)  41 us
    all_gather x1, blocking collectives, body(): lax.all_gather(local_vals, 'ctx', axis=0, tiled=True)  33.2 us
    ppermute x16, waiting for transfers between devices, passed_along(): return lax.ppermute(block, axis, route)  25.5 us
    unnamed x88, local copies, waits for them, and re-layouts  12.2 us
  transfers between devices with their start and end apart: 17, of which 6 were waited for; matrix products, arithmetic and copies ran while one was open for 7% of the time, Pallas kernels for 0%

commit v1 on v0

--- a/solution.py
+++ b/solution.py
@@ -6,6 +6,10 @@
 HEAD = 128
 BAND_LENGTH = 1024
 NEGATIVE = -1e30
+create_points = lambda inp, a_name, array_axis: jnp.concatenate(
+    lax.all_to_all(jnp.stack([inp for _ in range(lax.axis_size(a_name))]), a_name, 0, 0),
+    axis=array_axis,
+)
 
 
 def passed_along(block, axis, distance):
@@ -93,7 +97,7 @@
     local_keys = jnp.take(keys, local_rows, axis=0)
     local_vals = jnp.take(values, local_rows, axis=0)
     summ_keys, summ_vals = (
-        lax.all_gather(local_keys, "ctx", axis=0, tiled=True),
+        create_points(local_keys, "ctx", 0),
         lax.all_gather(local_vals, "ctx", axis=0, tiled=True),
     )
     query_pos = first_row + jnp.arange(row_count, dtype=jnp.int32)

time: 390 us -> 355 us (0.910)
  blocking collectives: 74.2 us -> 37 us
  starting transfers between devices: 43.8 us -> 50 us
    all_gather x1 -> x0, blocking collectives: 41 us -> none  [body(): lax.all_gather(local_keys, 'ctx', axis=0, tiled=True)]
    all_to_all x0 -> x1, starting transfers between devices: none -> 7.09 us  [lax.all_to_all(jnp.stack([inp for _ in range(lax.axis_size(a_name))]), a_...]
    unnamed x88 -> x91, local copies, waits for them, and re-layouts: 12.2 us -> 9.81 us
  transfers between devices with their start and end apart: 17 -> 18, of which waited for: 6 -> 5; matrix products, arithmetic and copies ran while one was open for 7% -> 7% of each run, Pallas kernels for 0% -> 0%
where the time goes in v1:
time: 355 us; the launch traced here: 354 us
  waiting for transfers between devices  167 us (47%)
  starting transfers between devices  50 us (14%)
  matrix products  41.2 us (12%)
  blocking collectives  37 us (10%)
  local copies, waits for them, and re-layouts  23.3 us (7%)
  other arithmetic  20.4 us (6%)
  between operations  15.3 us (4%)
    unnamed x2, waiting for transfers between devices  140 us
    ppermute x16, starting transfers between devices, passed_along(): return lax.ppermute(block, axis, route)  42.8 us
    all_gather x1, blocking collectives, body(): lax.all_gather(local_vals, 'ctx', axis=0, tiled=True)  37 us
    ppermute x16, waiting for transfers between devices, passed_along(): return lax.ppermute(block, axis, route)  27.1 us
    unnamed x91, local copies, waits for them, and re-layouts  9.81 us
  transfers between devices with their start and end apart: 18, of which 5 were waited for; matrix products, arithmetic and copies ran while one was open for 7% of the time, Pallas kernels for 0%

profile of v1, /device:TPU:1, one launch (start us, length us, event | category | flops | bytes accessed | tf_op | source)
XLA Modules:
  0.0 353.9 jit_solution(10718391613768321283)
XLA Ops:
  7.2 5.1 %collective-permute-start.3 = (bf16[256,512]{1,0:T(8,128)(2,1)}, bf16[256,512]{1,0:T(8,128)(2,1)}, u32[]{:S(2)}, u32[]{:S(2)}) collective-permute-start(bf16[256,512]{1,0:T(8,128)(2,1)} %param.8), channel_id=1, source_target_pairs={{0,1},{1,2},{2,3},{3,4},{4,5},{5,6},{6,7},{7,8},{8,9},{9,10},{10,1... | collective-permute-start | bytes 786440 | tf_op jit(solution)/shard_map/ppermute | solution.py:18
  12.3 4.2 %collective-permute-start.2 = (bf16[256,512]{1,0:T(8,128)(2,1)}, bf16[256,512]{1,0:T(8,128)(2,1)}, u32[]{:S(2)}, u32[]{:S(2)}) collective-permute-start(bf16[256,512]{1,0:T(8,128)(2,1)} %param.8), channel_id=1, source_target_pairs={{0,2},{1,3},{2,4},{3,5},{4,6},{5,7},{6,8},{7,9},{8,10},{9,11},{10,... | collective-permute-start | bytes 786440 | tf_op jit(solution)/shard_map/ppermute | solution.py:18
  16.5 3.3 collective-permute-start.6
  19.8 2.8 collective-permute-start.5
  22.5 4.3 %collective-permute-start.4 = (bf16[256,512]{1,0:T(8,128)(2,1)}, bf16[256,512]{1,0:T(8,128)(2,1)}, u32[]{:S(2)}, u32[]{:S(2)}) collective-permute-start(bf16[256,512]{1,0:T(8,128)(2,1)} %param.9), channel_id=1, source_target_pairs={{0,4},{1,5},{2,6},{3,7},{4,8},{5,9},{6,10},{7,11},{8,12},{9,13},{1... | collective-permute-start | bytes 786440 | tf_op jit(solution)/shard_map/ppermute | solution.py:18
  27.6 1.5 gather_fusion.1
  29.1 1.5 gather_fusion
  31.6 7.1 %all-to-all-start = ((bf16[128,2,512]{2,1,0:T(2,128)(2,1)}), bf16[128,2,512]{2,1,0:T(2,128)(2,1)S(1)}, u32[]{:S(2)}, u32[]{:S(2)}) async-start(bf16[128,2,512]{2,1,0:T(2,128)(2,1)} %stack.2), calls=%async_computation | async-start | bytes 524288 | tf_op jit(solution)/shard_map/all_to_all | solution.py:10
  38.8 2.0 fusion.97
  42.5 37.0 %all-gather = bf16[128,2,512]{2,1,0:T(2,128)(2,1)S(1)} all-gather(bf16[1,2,512]{2,1,0:T(2,128)(2,1)S(1)} %get-tuple-element.27), channel_id=1, replica_groups=mesh['ctx'=128] {'ctx'}, dimensions={0}, use_global_device_ids=true | all-gather | bytes 264192 | tf_op jit(solution)/shard_map/all_gather | solution.py:101
  79.6 1.2 copy.339
  83.4 2.9 collective-permute-start.7
  87.3 3.5 collective-permute-start.1
  91.8 3.5 %collective-permute-start = (bf16[256,512]{1,0:T(8,128)(2,1)S(1)}, bf16[256,512]{1,0:T(8,128)(2,1)S(1)}, u32[]{:S(2)}, u32[]{:S(2)}) collective-permute-start(bf16[256,512]{1,0:T(8,128)(2,1)S(1)} %copy-done.33), channel_id=1, source_target_pairs={{0,4},{1,5},{2,6},{3,7},{4,8},{5,9},{6,10},{7,11},{8,12},{9,13},{1... | collective-permute-start | bytes 786440 | tf_op jit(solution)/shard_map/ppermute | solution.py:18
  96.4 5.7 %collective-permute-done = bf16[256,512]{1,0:T(8,128)(2,1)S(1)} collective-permute-done((bf16[256,512]{1,0:T(8,128)(2,1)S(1)}, bf16[256,512]{1,0:T(8,128)(2,1)S(1)}, u32[]{:S(2)}, u32[]{:S(2)}) %collective-permute-start) | collective-permute-done | bytes 262176 | tf_op jit(solution)/shard_map/ppermute | solution.py:18
  106.0 1.0 convolution_bitcast_fusion.12
  107.4 1.0 fusion.50
  109.4 1.0 convolution_bitcast_fusion
  110.4 1.1 fusion.1
  113.7 1.0 convolution_bitcast_fusion.14
  114.7 1.0 fusion.52
  117.1 1.1 fusion.89
  118.2 1.0 convolution_bitcast_fusion.2
  119.2 1.1 fusion.5
  120.3 1.2 fusion.101
  124.0 1.0 fusion.51
  126.4 1.0 fusion.90
  127.4 1.0 convolution_bitcast_fusion.1
  128.5 1.1 fusion.3
  131.8 1.0 convolution_bitcast_fusion.15
  132.7 1.0 fusion.53
  134.2 1.0 fusion.54
  135.1 1.1 fusion.88
  136.2 1.0 convolution_bitcast_fusion.3
  137.2 1.1 fusion.7
  139.5 1.0 fusion.14
  140.5 1.2 fusion.13
  141.7 1.0 fusion.15
  142.6 1.2 fusion.94
  143.8 1.7 pad_maximum_fusion
  145.5 1.2 fusion.93
  146.7 1.7 pad_maximum_fusion.1
  149.8 1.5 fusion.43
  152.2 2.7 fusion.44
  155.7 1.5 fusion.42
  157.4 2.3 fusion.96
  159.8 1.3 collective-permute-start.8
  161.1 2.6 collective-permute-start.11
  163.7 1.3 collective-permute-start.10
  165.0 1.4 collective-permute-start.9
  166.5 1.0 fusion.95
  167.5 1.4 collective-permute-start.12
  169.0 2.0 pad_maximum_fusion.3
  171.0 1.1 pad_maximum_fusion.2
  172.1 2.7 collective-permute-start.15
  174.9 4.1 %collective-permute-done.11 = bf16[256,512]{0,1:T(8,128)(2,1)} collective-permute-done((bf16[256,512]{0,1:T(8,128)(2,1)}, bf16[256,512]{0,1:T(8,128)(2,1)}, u32[]{:S(2)}, u32[]{:S(2)}) %collective-permute-start.11) | collective-permute-done | bytes 262176 | tf_op jit(solution)/shard_map/ppermute | solution.py:18
  179.0 1.3 collective-permute-start.14
  180.3 1.3 collective-permute-start.13
  181.6 1.5 fusion.75
  183.3 16.7 %collective-permute-done.15 = bf16[256,512]{0,1:T(8,128)(2,1)S(1)} collective-permute-done((bf16[256,512]{0,1:T(8,128)(2,1)}, bf16[256,512]{0,1:T(8,128)(2,1)S(1)}, u32[]{:S(2)}, u32[]{:S(2)}) %collective-permute-start.15) | collective-permute-done | bytes 262176 | tf_op jit(solution)/shard_map/ppermute | solution.py:18
  200.5 1.2 fusion.72
  201.9 139.6 %all-reduce.5.cloned.1.call-done = (f32[256,512]{0,1:T(8,128)}, f32[256,512]{0,1:T(8,128)}) async-done(((f32[256,512]{0,1:T(8,128)}, f32[256,512]{0,1:T(8,128)}), (f32[256,512]{0,1:T(8,128)}, f32[256,512]{0,1:T(8,128)})) %all-reduce.5.cloned.1.call-update) | async-done | bytes 1048592
  341.5 1.1 constant_dynamic-slice_fusion.1
  342.5 1.1 constant_dynamic-slice_fusion
  (171 shorter events, 32.6 us)
Async XLA Ops:
  7.2 33.6 %copy-start.21 = (bf16[256,2048]{1,0:T(8,128)(2,1)S(1)}, bf16[256,2048]{1,0:T(8,128)(2,1)}, u32[]{:S(2)}) copy-start(bf16[256,2048]{1,0:T(8,128)(2,1)} %param.10) | copy-start | bytes 3145732
  7.2 96.0 %collective-permute-start.3 = (bf16[256,512]{1,0:T(8,128)(2,1)}, bf16[256,512]{1,0:T(8,128)(2,1)}, u32[]{:S(2)}, u32[]{:S(2)}) collective-permute-start(bf16[256,512]{1,0:T(8,128)(2,1)} %param.8), channel_id=1, source_target_pairs={{0,1},{1,2},{2,3},{3,4},{4,5},{5,6},{6,7},{7,8},{8,9},{9,10},{10,1... | collective-permute-start | bytes 786440 | tf_op jit(solution)/shard_map/ppermute | solution.py:18
  12.3 89.9 %collective-permute-start.2 = (bf16[256,512]{1,0:T(8,128)(2,1)}, bf16[256,512]{1,0:T(8,128)(2,1)}, u32[]{:S(2)}, u32[]{:S(2)}) collective-permute-start(bf16[256,512]{1,0:T(8,128)(2,1)} %param.8), channel_id=1, source_target_pairs={{0,2},{1,3},{2,4},{3,5},{4,6},{5,7},{6,8},{7,9},{8,10},{9,11},{10,... | collective-permute-start | bytes 786440 | tf_op jit(solution)/shard_map/ppermute | solution.py:18
  16.5 75.3 %collective-permute-start.6 = (bf16[256,512]{1,0:T(8,128)(2,1)}, bf16[256,512]{1,0:T(8,128)(2,1)}, u32[]{:S(2)}, u32[]{:S(2)}) collective-permute-start(bf16[256,512]{1,0:T(8,128)(2,1)} %param.9), channel_id=1, source_target_pairs={{0,2},{1,3},{2,4},{3,5},{4,6},{5,7},{6,8},{7,9},{8,10},{9,11},{10,... | collective-permute-start | bytes 786440 | tf_op jit(solution)/shard_map/ppermute | solution.py:18
  19.8 67.5 %collective-permute-start.5 = (bf16[256,512]{1,0:T(8,128)(2,1)}, bf16[256,512]{1,0:T(8,128)(2,1)}, u32[]{:S(2)}, u32[]{:S(2)}) collective-permute-start(bf16[256,512]{1,0:T(8,128)(2,1)} %param.9), channel_id=1, source_target_pairs={{0,3},{1,4},{2,5},{3,6},{4,7},{5,8},{6,9},{7,10},{8,11},{9,12},{10... | collective-permute-start | bytes 786440 | tf_op jit(solution)/shard_map/ppermute | solution.py:18
  22.5 60.9 %collective-permute-start.4 = (bf16[256,512]{1,0:T(8,128)(2,1)}, bf16[256,512]{1,0:T(8,128)(2,1)}, u32[]{:S(2)}, u32[]{:S(2)}) collective-permute-start(bf16[256,512]{1,0:T(8,128)(2,1)} %param.9), channel_id=1, source_target_pairs={{0,4},{1,5},{2,6},{3,7},{4,8},{5,9},{6,10},{7,11},{8,12},{9,13},{1... | collective-permute-start | bytes 786440 | tf_op jit(solution)/shard_map/ppermute | solution.py:18
  31.6 50.4 %all-to-all-start = ((bf16[128,2,512]{2,1,0:T(2,128)(2,1)}), bf16[128,2,512]{2,1,0:T(2,128)(2,1)S(1)}, u32[]{:S(2)}, u32[]{:S(2)}) async-start(bf16[128,2,512]{2,1,0:T(2,128)(2,1)} %stack.2), calls=%async_computation | async-start | bytes 524288 | tf_op jit(solution)/shard_map/all_to_all | solution.py:10
  38.7 302.8 %all-reduce.5.cloned.1.call-start = ((), (), s32[]{:S(2)}) async-start(), calls=%async_computation.1 | async-start | bytes 2097152
  41.6 40.3 %copy-start.35 = (s32[256]{0:T(256)S(1)}, s32[256]{0:T(256)}, u32[]{:S(2)}) copy-start(s32[256]{0:T(256)} %param.11) | copy-start | bytes 3076
  42.5 69.0 %copy-start.3 = (pred[256,1280]{0,1:T(8,128)(4,1)}, pred[256,1280]{0,1:T(8,128)(4,1)S(1)}, u32[]{:S(2)}) copy-start(pred[256,1280]{0,1:T(8,128)(4,1)S(1)} %fusion.33) | copy-start | bytes 983044
  79.6 36.2 %copy-start.17 = (bf16[256,512]{1,0:T(8,128)(2,1)}, bf16[256,512]{1,0:T(8,128)(2,1)S(1)}, u32[]{:S(2)}) copy-start(bf16[256,512]{1,0:T(8,128)(2,1)S(1)} %reshape.259) | copy-start | bytes 786436
  79.6 1.9 copy-start.25
  80.8 2.3 copy-start.5
  81.0 1.8 copy-start.7
  81.1 35.0 %copy-start.9 = (bf16[256,512]{0,1:T(8,128)(2,1)}, bf16[256,512]{0,1:T(8,128)(2,1)S(1)}, u32[]{:S(2)}) copy-start(bf16[256,512]{0,1:T(8,128)(2,1)S(1)} %copy.342) | copy-start | bytes 786436
  81.3 27.5 %copy-start.11 = (bf16[256,512]{0,1:T(8,128)(2,1)}, bf16[256,512]{0,1:T(8,128)(2,1)S(1)}, u32[]{:S(2)}) copy-start(bf16[256,512]{0,1:T(8,128)(2,1)S(1)} %copy.348) | copy-start | bytes 786436
  82.1 35.0 %copy-start.15 = (bf16[256,512]{1,0:T(8,128)(2,1)}, bf16[256,512]{1,0:T(8,128)(2,1)S(1)}, u32[]{:S(2)}) copy-start(bf16[256,512]{1,0:T(8,128)(2,1)S(1)} %reshape.210) | copy-start | bytes 786436
  82.1 1.3 copy-start.32
  82.5 4.8 %copy-start.33 = (bf16[256,512]{1,0:T(8,128)(2,1)S(1)}, bf16[256,512]{1,0:T(8,128)(2,1)}, u32[]{:S(2)}) copy-start(bf16[256,512]{1,0:T(8,128)(2,1)} %param.8) | copy-start | bytes 786436
  83.4 12.9 %collective-permute-start.7 = (bf16[256,512]{1,0:T(8,128)(2,1)S(1)}, bf16[256,512]{1,0:T(8,128)(2,1)S(1)}, u32[]{:S(2)}, u32[]{:S(2)}) collective-permute-start(bf16[256,512]{1,0:T(8,128)(2,1)S(1)} %copy-done.32), channel_id=1, source_target_pairs={{0,1},{1,2},{2,3},{3,4},{4,5},{5,6},{6,7},{7,8},{8,9},{9,10},{10,1... | collective-permute-start | bytes 786440 | tf_op jit(solution)/shard_map/ppermute | solution.py:18
  87.3 14.8 %collective-permute-start.1 = (bf16[256,512]{1,0:T(8,128)(2,1)S(1)}, bf16[256,512]{1,0:T(8,128)(2,1)S(1)}, u32[]{:S(2)}, u32[]{:S(2)}) collective-permute-start(bf16[256,512]{1,0:T(8,128)(2,1)S(1)} %copy-done.33), channel_id=1, source_target_pairs={{0,3},{1,4},{2,5},{3,6},{4,7},{5,8},{6,9},{7,10},{8,11},{9,12},{10... | collective-permute-start | bytes 786440 | tf_op jit(solution)/shard_map/ppermute | solution.py:18
  91.8 10.3 %collective-permute-start = (bf16[256,512]{1,0:T(8,128)(2,1)S(1)}, bf16[256,512]{1,0:T(8,128)(2,1)S(1)}, u32[]{:S(2)}, u32[]{:S(2)}) collective-permute-start(bf16[256,512]{1,0:T(8,128)(2,1)S(1)} %copy-done.33), channel_id=1, source_target_pairs={{0,4},{1,5},{2,6},{3,7},{4,8},{5,9},{6,10},{7,11},{8,12},{9,13},{1... | collective-permute-start | bytes 786440 | tf_op jit(solution)/shard_map/ppermute | solution.py:18
  104.2 44.2 %copy-start.13 = (bf16[1280,512]{1,0:T(8,128)(2,1)}, bf16[1280,512]{1,0:T(8,128)(2,1)S(1)}, u32[]{:S(2)}) copy-start(bf16[1280,512]{1,0:T(8,128)(2,1)S(1)} %constant_dynamic-update-slice_fusion) | copy-start | bytes 3932164
  119.2 1.1 copy-start.4
  119.2 1.1 copy-start.8
  121.7 1.0 copy-start.18
  125.0 1.4 copy-start.16
  128.5 1.1 copy-start.6
  129.5 10.9 %copy-start = (bf16[4,256,1280]{1,2,0:T(8,128)(2,1)}, bf16[4,256,1280]{1,2,0:T(8,128)(2,1)S(1)}, u32[]{:S(2)}) copy-start(bf16[4,256,1280]{1,2,0:T(8,128)(2,1)S(1)} %fusion.3) | copy-start | bytes 7864324
  137.2 1.1 copy-start.12
  138.3 3.3 copy-start.1
  138.3 1.1 copy-start.10
  148.4 1.4 copy-start.19
  151.3 4.4 %copy-start.2 = (bf16[4,256,1280]{1,2,0:T(8,128)(2,1)S(1)}, bf16[4,256,1280]{1,2,0:T(8,128)(2,1)}, u32[]{:S(2)}) copy-start(bf16[4,256,1280]{1,2,0:T(8,128)(2,1)} %copy-done.1) | copy-start | bytes 7864324
  151.3 4.4 %copy-start.20 = (f32[128,4,256]{2,0,1:T(8,128)S(1)}, f32[128,4,256]{2,0,1:T(8,128)}, u32[]{:S(2)}) copy-start(f32[128,4,256]{2,0,1:T(8,128)} %fusion.88) | copy-start | bytes 1572868
  157.2 9.2 %copy-start.14 = (bf16[1280,512]{0,1:T(8,128)(2,1)S(1)}, bf16[1280,512]{0,1:T(8,128)(2,1)}, u32[]{:S(2)}) copy-start(bf16[1280,512]{0,1:T(8,128)(2,1)} %fusion.93) | copy-start | bytes 3932164
  157.2 11.7 %copy-start.26 = (f32[256,128]{0,1:T(8,128)S(1)}, f32[256,128]{0,1:T(8,128)}, u32[]{:S(2)}) copy-start(f32[256,128]{0,1:T(8,128)} %fusion.55) | copy-start | bytes 393220
  157.2 11.7 %copy-start.27 = (f32[256,128]{0,1:T(8,128)S(1)}, f32[256,128]{0,1:T(8,128)}, u32[]{:S(2)}) copy-start(f32[256,128]{0,1:T(8,128)} %fusion.56) | copy-start | bytes 393220
  157.3 11.7 %copy-start.28 = (f32[256,128]{0,1:T(8,128)S(1)}, f32[256,128]{0,1:T(8,128)}, u32[]{:S(2)}) copy-start(f32[256,128]{0,1:T(8,128)} %fusion.54) | copy-start | bytes 393220
  157.3 11.7 %copy-start.29 = (f32[256,128]{0,1:T(8,128)S(1)}, f32[256,128]{0,1:T(8,128)}, u32[]{:S(2)}) copy-start(f32[256,128]{0,1:T(8,128)} %convolution_bitcast_fusion.12) | copy-start | bytes 393220
  157.3 11.7 %copy-start.30 = (f32[256,128]{0,1:T(8,128)S(1)}, f32[256,128]{0,1:T(8,128)}, u32[]{:S(2)}) copy-start(f32[256,128]{0,1:T(8,128)} %convolution_bitcast_fusion.14) | copy-start | bytes 393220
  157.3 11.7 %copy-start.31 = (f32[256,128]{0,1:T(8,128)S(1)}, f32[256,128]{0,1:T(8,128)}, u32[]{:S(2)}) copy-start(f32[256,128]{0,1:T(8,128)} %convolution_bitcast_fusion.13) | copy-start | bytes 393220
  159.8 12.3 %collective-permute-start.8 = (bf16[256,512]{0,1:T(8,128)(2,1)}, bf16[256,512]{0,1:T(8,128)(2,1)}, u32[]{:S(2)}, u32[]{:S(2)}) collective-permute-start(bf16[256,512]{0,1:T(8,128)(2,1)} %get-tuple-element.15), channel_id=1, source_target_pairs={{4,0},{5,1},{6,2},{7,3},{8,4},{9,5},{10,6},{11,7},{12,8},{13,9},{1... | collective-permute-start | bytes 786440 | tf_op jit(solution)/shard_map/ppermute | solution.py:18
  161.1 17.9 %collective-permute-start.11 = (bf16[256,512]{0,1:T(8,128)(2,1)}, bf16[256,512]{0,1:T(8,128)(2,1)}, u32[]{:S(2)}, u32[]{:S(2)}) collective-permute-start(bf16[256,512]{0,1:T(8,128)(2,1)} %get-tuple-element.16), channel_id=1, source_target_pairs={{1,0},{2,1},{3,2},{4,3},{5,4},{6,5},{7,6},{8,7},{9,8},{10,9},{11,1... | collective-permute-start | bytes 786440 | tf_op jit(solution)/shard_map/ppermute | solution.py:18
  163.7 16.6 %collective-permute-start.10 = (bf16[256,512]{0,1:T(8,128)(2,1)}, bf16[256,512]{0,1:T(8,128)(2,1)}, u32[]{:S(2)}, u32[]{:S(2)}) collective-permute-start(bf16[256,512]{0,1:T(8,128)(2,1)} %get-tuple-element.17), channel_id=1, source_target_pairs={{2,0},{3,1},{4,2},{5,3},{6,4},{7,5},{8,6},{9,7},{10,8},{11,9},{12,... | collective-permute-start | bytes 786440 | tf_op jit(solution)/shard_map/ppermute | solution.py:18
  165.0 6.0 %copy-start.22 = (bf16[256,512]{1,0:T(8,128)(2,1)S(1)}, bf16[256,512]{1,0:T(8,128)(2,1)}, u32[]{:S(2)}) copy-start(bf16[256,512]{1,0:T(8,128)(2,1)} %copy.234) | copy-start | bytes 786436
  165.0 6.0 %copy-start.23 = (bf16[256,512]{1,0:T(8,128)(2,1)S(1)}, bf16[256,512]{1,0:T(8,128)(2,1)}, u32[]{:S(2)}) copy-start(bf16[256,512]{1,0:T(8,128)(2,1)} %copy.232) | copy-start | bytes 786436
  165.0 6.0 %copy-start.24 = (bf16[256,512]{1,0:T(8,128)(2,1)S(1)}, bf16[256,512]{1,0:T(8,128)(2,1)}, u32[]{:S(2)}) copy-start(bf16[256,512]{1,0:T(8,128)(2,1)} %copy.233) | copy-start | bytes 786436
  165.0 16.6 %collective-permute-start.9 = (bf16[256,512]{0,1:T(8,128)(2,1)}, bf16[256,512]{0,1:T(8,128)(2,1)}, u32[]{:S(2)}, u32[]{:S(2)}) collective-permute-start(bf16[256,512]{0,1:T(8,128)(2,1)} %get-tuple-element.18), channel_id=1, source_target_pairs={{3,0},{4,1},{5,2},{6,3},{7,4},{8,5},{9,6},{10,7},{11,8},{12,9},{13... | collective-permute-start | bytes 786440 | tf_op jit(solution)/shard_map/ppermute | solution.py:18
  167.5 12.8 %copy-start.34 = (bf16[256,512]{0,1:T(8,128)(2,1)S(1)}, bf16[256,512]{0,1:T(8,128)(2,1)}, u32[]{:S(2)}) copy-start(bf16[256,512]{0,1:T(8,128)(2,1)} %get-tuple-element.14) | copy-start | bytes 786436
  167.5 15.8 %collective-permute-start.12 = (bf16[256,512]{0,1:T(8,128)(2,1)}, bf16[256,512]{0,1:T(8,128)(2,1)S(1)}, u32[]{:S(2)}, u32[]{:S(2)}) collective-permute-start(bf16[256,512]{0,1:T(8,128)(2,1)} %get-tuple-element.11), channel_id=1, source_target_pairs={{4,0},{5,1},{6,2},{7,3},{8,4},{9,5},{10,6},{11,7},{12,8},{13,9},{1... | collective-permute-start | bytes 786440 | tf_op jit(solution)/shard_map/ppermute | solution.py:18
  172.1 27.9 %collective-permute-start.15 = (bf16[256,512]{0,1:T(8,128)(2,1)}, bf16[256,512]{0,1:T(8,128)(2,1)S(1)}, u32[]{:S(2)}, u32[]{:S(2)}) collective-permute-start(bf16[256,512]{0,1:T(8,128)(2,1)} %get-tuple-element.12), channel_id=1, source_target_pairs={{1,0},{2,1},{3,2},{4,3},{5,4},{6,5},{7,6},{8,7},{9,8},{10,9},{11,1... | collective-permute-start | bytes 786440 | tf_op jit(solution)/shard_map/ppermute | solution.py:18
  179.0 21.5 %collective-permute-start.14 = (bf16[256,512]{0,1:T(8,128)(2,1)}, bf16[256,512]{0,1:T(8,128)(2,1)S(1)}, u32[]{:S(2)}, u32[]{:S(2)}) collective-permute-start(bf16[256,512]{0,1:T(8,128)(2,1)} %get-tuple-element.13), channel_id=1, source_target_pairs={{2,0},{3,1},{4,2},{5,3},{6,4},{7,5},{8,6},{9,7},{10,8},{11,9},{12,... | collective-permute-start | bytes 786440 | tf_op jit(solution)/shard_map/ppermute | solution.py:18
  180.3 20.2 %collective-permute-start.13 = (bf16[256,512]{0,1:T(8,128)(2,1)S(1)}, bf16[256,512]{0,1:T(8,128)(2,1)S(1)}, u32[]{:S(2)}, u32[]{:S(2)}) collective-permute-start(bf16[256,512]{0,1:T(8,128)(2,1)S(1)} %copy-done.34), channel_id=1, source_target_pairs={{3,0},{4,1},{5,2},{6,3},{7,4},{8,5},{9,6},{10,7},{11,8},{12,9},{13... | collective-permute-start | bytes 786440 | tf_op jit(solution)/shard_map/ppermute | solution.py:18
Sparse Core Ops, SparseCore 0:
  171.1 170.3 all-reduce.4
